TPU v7x, 32 devices: a whole 2x2x4 slice. The times are simulated.
32 devices in a mesh: groups: 2 (over y), seq: 4 (over z), head: 4 (over x, core).
Axes of the slice: x: 2, y: 2, z: 4, core: 2. Of those that a mesh axis runs over, the one named last changes fastest.
Arguments:
- query: bfloat16 [8192, 1536], P(('groups', 'seq', 'head')), parts along dimension 0, may hold values from -150 to 150
- key_in: bfloat16 [8192, 1536], P(('groups', 'seq', 'head')), parts along dimension 0, may hold values from -6 to 6
- value: bfloat16 [8192, 1536], P(('groups', 'seq', 'head')), parts along dimension 0, may hold values from -6 to 6
- grad_out: bfloat16 [8192, 1536], P(('groups', 'seq', 'head')), parts along dimension 0, may hold values from -6 to 6
- pattern: int32 [16, 3], replicated, may hold values from 0 to 15, as said below
- live: int32 [16, 3], replicated, may hold values from 0 to 1, as said below
Outputs:
- attended: bfloat16 [8192, 1536], P(('groups', 'seq', 'head')), parts along dimension 0
- query_grad: bfloat16 [8192, 1536], P(('groups', 'seq', 'head')), parts along dimension 0
- key_grad: bfloat16 [8192, 1536], P(('groups', 'seq', 'head')), parts along dimension 0
- value_grad: bfloat16 [8192, 1536], P(('groups', 'seq', 'head')), parts along dimension 0
There are 2 independent parts, one for each index of `groups`. A program takes and returns all parts, laid end to end along the dimension named above; an argument that names none is the same for every part. Nothing has to cross between parts.
Inputs may be any that keep to these rules, and one draw needn't show every extreme that they name: `pattern`: each entry names a tile of the same frame-tile layer as its query tile or of the layer just before or after it; the live entries of a row are distinct; an entry that is not live names the query tile itself. Slot 0 of every row is live and names the query tile itself.
All inputs are finite; a program needn't handle non-finite values.
Results may differ from a plain program's by a relative error of at most 0.015.
Values may be sent and summed in bfloat16 or wider, within the bound.
A program may use at most 128 MiB of HBM per device.

v0:
```python
import jax
import jax.numpy as jnp
from jax import lax
from jax.sharding import PartitionSpec as P

HEADS = 12
HEAD_DIM = 128


def extended_2(cells, sides, width):
    for axis, dim in sides:
        count = lax.axis_size(axis)
        ends = count - 1
        head = lax.slice_in_dim(cells, 0, width, axis=dim)
        tail = lax.slice_in_dim(cells, cells.shape[dim] - width, cells.shape[dim], axis=dim)
        cells = jnp.concatenate(
            [
                lax.ppermute(tail, axis, [(i, (i + 1) % count) for i in range(ends)]),
                cells,
                lax.ppermute(head, axis, [((i + 1) % count, i) for i in range(ends)]),
            ],
            axis=dim,
        )
    return cells


def shifted(value, axis, steps):
    count = lax.axis_size(axis)
    initial, last = (max(0, -steps), min(count, count - steps))
    return lax.ppermute(value, axis, [(source, source + steps) for source in range(initial, last)])


def head_split(rows_flat, tiles, heads):
    width = rows_flat.shape[1]
    return rows_flat.reshape(tiles, rows_flat.shape[0] // tiles, heads, width // heads).transpose(
        2, 0, 1, 3
    )


def head_join(blocks):
    heads, tiles, tile_size, head_size = blocks.shape
    return blocks.transpose(1, 2, 0, 3).reshape(tiles * tile_size, heads * head_size)


def forward_head(q_tile, g_tile, k_all, v_all, tile_ids, alive, scale):
    k_sel = k_all[tile_ids]
    v_sel = v_all[tile_ids]
    scores = jnp.einsum("aqd,ankd->aqnk", q_tile, k_sel, preferred_element_type=jnp.float32) * scale
    scores = jnp.where(alive[:, None, :, None], scores, -jnp.inf)
    peak = jnp.max(scores, axis=(2, 3), keepdims=True)
    exponent = jnp.exp(scores - peak)
    total = jnp.sum(exponent, axis=(2, 3), keepdims=True)
    weights = exponent / total
    weights_low = weights.astype(jnp.bfloat16)
    attended = jnp.einsum(
        "aqnk,ankd->aqd", weights_low, v_sel, preferred_element_type=jnp.float32
    ).astype(jnp.bfloat16)
    weight_grad = jnp.einsum("aqd,ankd->aqnk", g_tile, v_sel, preferred_element_type=jnp.float32)
    delta = jnp.sum(weights * weight_grad, axis=(2, 3), keepdims=True)
    score_grad = (weights * (weight_grad - delta) * scale).astype(jnp.bfloat16)
    query_grad = jnp.einsum(
        "aqnk,ankd->aqd", score_grad, k_sel, preferred_element_type=jnp.float32
    ).astype(jnp.bfloat16)
    onehot = (
        tile_ids[:, :, None] == jnp.arange(k_all.shape[0], dtype=jnp.int32)[None, None, :]
    ).astype(jnp.float32)
    key_slots = jnp.einsum("aqnk,aqd->ankd", score_grad, q_tile, preferred_element_type=jnp.float32)
    value_slots = jnp.einsum(
        "aqnk,aqd->ankd", weights_low, g_tile, preferred_element_type=jnp.float32
    )
    key_sums = jnp.einsum("anj,ankd->jkd", onehot, key_slots, precision=lax.Precision.HIGHEST)
    value_sums = jnp.einsum("anj,ankd->jkd", onehot, value_slots, precision=lax.Precision.HIGHEST)
    return (attended, query_grad, key_sums, value_sums)


def body(query, key_in, value, grad_out, pattern, live):
    members = lax.axis_size("head")
    heads = HEADS // members
    scale = HEAD_DIM ** (-0.5)
    queries, keys, values, out_grads = (
        lax.all_to_all(query, "head", split_axis=1, concat_axis=0, tiled=True),
        lax.all_to_all(key_in, "head", split_axis=1, concat_axis=0, tiled=True),
        lax.all_to_all(value, "head", split_axis=1, concat_axis=0, tiled=True),
        lax.all_to_all(grad_out, "head", split_axis=1, concat_axis=0, tiled=True),
    )
    tile_size = queries.shape[0] // members
    margin = members * tile_size
    seq_index = lax.axis_index("seq")
    first = seq_index * members
    extended = extended_2(jnp.stack([keys, values]), (("seq", 1),), margin)
    rows = lax.dynamic_slice_in_dim(pattern, first, members, 0)
    alive_rows = lax.dynamic_slice_in_dim(live, first, members, 0)
    tile_ids = rows - first + members
    alive = alive_rows > 0
    q_heads = head_split(queries, members, heads)
    g_heads = head_split(out_grads, members, heads)
    k_heads = head_split(extended[0], 3 * members, heads)
    v_heads = head_split(extended[1], 3 * members, heads)

    def with_partials(operands):
        return forward_head(
            operands[0], operands[1], operands[2], operands[3], tile_ids, alive, scale
        )

    attended, query_grad, key_sums, value_sums = lax.map(
        with_partials, (q_heads, g_heads, k_heads, v_heads)
    )
    grads = jnp.stack([head_join(key_sums), head_join(value_sums)])
    from_above = shifted(grads[:, :margin].astype(jnp.bfloat16), "seq", -1).astype(jnp.float32)
    from_below = shifted(grads[:, 2 * margin :].astype(jnp.bfloat16), "seq", 1).astype(jnp.float32)
    owned = grads[:, margin : 2 * margin] + from_above + from_below
    key_own = owned[0]
    value_own = owned[1]
    result = (
        lax.all_to_all(head_join(attended), "head", split_axis=0, concat_axis=1, tiled=True),
        lax.all_to_all(head_join(query_grad), "head", split_axis=0, concat_axis=1, tiled=True),
        lax.all_to_all(
            key_own.astype(jnp.bfloat16), "head", split_axis=0, concat_axis=1, tiled=True
        ),
        lax.all_to_all(
            value_own.astype(jnp.bfloat16), "head", split_axis=0, concat_axis=1, tiled=True
        ),
    )
    return (result[0], result[1], result[2], result[3])


def solution(mesh):
    placed = (
        P(("groups", "seq", "head"), None),
        P(("groups", "seq", "head"), None),
        P(("groups", "seq", "head"), None),
        P(("groups", "seq", "head"), None),
        P(),
        P(),
    )
    return jax.shard_map(
        body,
        mesh=mesh,
        in_specs=placed,
        out_specs=(
            P(("groups", "seq", "head"), None),
            P(("groups", "seq", "head"), None),
            P(("groups", "seq", "head"), None),
            P(("groups", "seq", "head"), None),
        ),
        check_vma=False,
    )
```

profile of v0, /device:TPU:24, one launch (start us, length us, event | category | flops | bytes accessed | tf_op | source)
XLA Modules:
  0.0 323.6 jit_solution(741371311791878829)
XLA Ops:
  0.6 2.4 copy.43
  3.0 3.5 %all-to-all-start.1 = ((bf16[256,4,384]{0,2,1:T(8,128)(2,1)}), bf16[256,4,384]{0,2,1:T(8,128)(2,1)S(1)}, u32[]{:S(2)}, u32[]{:S(2)}) async-start(bf16[256,4,384]{0,2,1:T(8,128)(2,1)} %bitcast.30), calls=%async_computation.1 | async-start | bytes 1572864 | tf_op jit(solution)/shard_map/all_to_all | solution.py:82
  7.7 10.5 %all-to-all-done.1 = bf16[256,4,384]{0,2,1:T(8,128)(2,1)S(1)} async-done(((bf16[256,4,384]{0,2,1:T(8,128)(2,1)}), bf16[256,4,384]{0,2,1:T(8,128)(2,1)S(1)}, u32[]{:S(2)}, u32[]{:S(2)}) %all-to-all-start.1) | async-done | bytes 786464 | tf_op jit(solution)/shard_map/all_to_all | solution.py:82
  18.1 3.5 %all-to-all-start.2 = ((bf16[256,4,384]{0,2,1:T(8,128)(2,1)}), bf16[256,4,384]{0,2,1:T(8,128)(2,1)S(1)}, u32[]{:S(2)}, u32[]{:S(2)}) async-start(bf16[256,4,384]{0,2,1:T(8,128)(2,1)} %bitcast.33), calls=%async_computation.2 | async-start | bytes 1572864 | tf_op jit(solution)/shard_map/all_to_all | solution.py:83
  22.0 11.2 %all-to-all-done.2 = bf16[256,4,384]{0,2,1:T(8,128)(2,1)S(1)} async-done(((bf16[256,4,384]{0,2,1:T(8,128)(2,1)}), bf16[256,4,384]{0,2,1:T(8,128)(2,1)S(1)}, u32[]{:S(2)}, u32[]{:S(2)}) %all-to-all-start.2) | async-done | bytes 786464 | tf_op jit(solution)/shard_map/all_to_all | solution.py:83
  35.0 3.5 %collective-permute-start.1 = (bf16[2,1024,384]{2,1,0:T(8,128)(2,1)}, bf16[2,1024,384]{2,1,0:T(8,128)(2,1)}, u32[]{:S(2)}, u32[]{:S(2)}) collective-permute-start(bf16[2,1024,384]{2,1,0:T(8,128)(2,1)} %pad_maximum_fusion.1), channel_id=1, source_target_pairs={{4,0},{8,4},{12,8},{5,1},{9,5},{13,9},{6,2},{10,6},{14,10},{7,3},{... | collective-permute-start | bytes 4718600 | tf_op jit(solution)/shard_map/ppermute | solution.py:20
  40.9 3.5 %all-to-all-start = ((bf16[256,4,384]{0,2,1:T(8,128)(2,1)}), bf16[256,4,384]{0,2,1:T(8,128)(2,1)S(1)}, u32[]{:S(2)}, u32[]{:S(2)}) async-start(bf16[256,4,384]{0,2,1:T(8,128)(2,1)} %bitcast.26), calls=%async_computation | async-start | bytes 1572864 | tf_op jit(solution)/shard_map/all_to_all | solution.py:81
  45.9 25.2 %collective-permute-done.1 = bf16[2,1024,384]{2,1,0:T(8,128)(2,1)} collective-permute-done((bf16[2,1024,384]{2,1,0:T(8,128)(2,1)}, bf16[2,1024,384]{2,1,0:T(8,128)(2,1)}, u32[]{:S(2)}, u32[]{:S(2)}) %collective-permute-start.1) | collective-permute-done | bytes 1572896 | tf_op jit(solution)/shard_map/ppermute | solution.py:20
  71.1 5.2 %collective-permute-done = bf16[2,1024,384]{2,1,0:T(8,128)(2,1)} collective-permute-done((bf16[2,1024,384]{2,1,0:T(8,128)(2,1)}, bf16[2,1024,384]{2,1,0:T(8,128)(2,1)}, u32[]{:S(2)}, u32[]{:S(2)}) %collective-permute-start) | collective-permute-done | bytes 1572896 | tf_op jit(solution)/shard_map/ppermute | solution.py:18
  76.3 4.6 %pad_maximum_fusion = bf16[2,3072,384]{2,1,0:T(8,128)(2,1)} fusion(bf16[2,1024,384]{2,1,0:T(8,128)(2,1)} %collective-permute-done.1, bf16[1,1024,384]{2,1,0:T(8,128)(2,1)S(1)} %bitcast.172, bf16[1,1024,384]{2,1,0:T(8,128)(2,1)S(1)} %bitcast.170, bf16[2,1024,384]{2,1,0:T(8,128)(2,1)} %collective-permute-done), kind=kLoop, calls=%fused_computation.47 | loop fusion | flops 18874368 | bytes 9437184 | tf_op jit(solution)/shard_map/concatenate | solution.py:16
  81.0 4.2 %all-to-all-start.3 = ((bf16[256,4,384]{0,2,1:T(8,128)(2,1)}), bf16[256,4,384]{0,2,1:T(8,128)(2,1)}, u32[]{:S(2)}, u32[]{:S(2)}) async-start(bf16[256,4,384]{0,2,1:T(8,128)(2,1)} %bitcast.38), calls=%async_computation.3 | async-start | bytes 1572864 | tf_op jit(solution)/shard_map/all_to_all | solution.py:84
  85.2 4.3 %fusion.37 = (bf16[1,3072,384]{2,1,0:T(8,128)(2,1)}, bf16[1,3072,384]{2,1,0:T(8,128)(2,1)S(1)}) fusion(bf16[2,3072,384]{2,1,0:T(8,128)(2,1)} %pad_maximum_fusion), kind=kLoop, calls=%fused_computation.59 | loop fusion | bytes 9437184 | tf_op jit(solution)/shard_map/slice | solution.py:98
  89.4 4.3 %copy.49 = bf16[1,3072,384]{1,2,0:T(8,128)(2,1)} copy(bf16[1,3072,384]{2,1,0:T(8,128)(2,1)} %get-tuple-element.128) | data formatting | bytes 4718592 | tf_op jit(solution)/shard_map/slice | solution.py:98
  93.7 5.4 %reshape_squeeze.7 = bf16[12,256,3,128]{1,0,3,2:T(8,128)(2,1)} reshape(bf16[1,3072,384]{1,2,0:T(8,128)(2,1)} %copy.49) | data formatting | bytes 4718592 | tf_op jit(solution)/shard_map/reshape;squeeze | solution.py:35
  99.1 4.8 %copy.53 = bf16[3,12,256,128]{3,2,1,0:T(8,128)(2,1)} copy(bf16[3,12,256,128]{2,1,3,0:T(8,128)(2,1)} %bitcast.167) | data formatting | bytes 4718592 | tf_op jit(solution)/shard_map/while | solution.py:105
  103.9 2.7 copy.47
  106.6 5.4 %reshape_squeeze.6 = bf16[12,256,3,128]{1,0,3,2:T(8,128)(2,1)} reshape(bf16[1,3072,384]{1,2,0:T(8,128)(2,1)} %copy.47) | data formatting | bytes 4718592 | tf_op jit(solution)/shard_map/reshape;squeeze | solution.py:35
  112.0 4.8 %copy.52 = bf16[3,12,256,128]{3,2,1,0:T(8,128)(2,1)} copy(bf16[3,12,256,128]{2,1,3,0:T(8,128)(2,1)} %bitcast.168) | data formatting | bytes 4718592 | tf_op jit(solution)/shard_map/while | solution.py:105
  116.8 92.5 %while.16 = (s32[]{:T(128)}, bf16[3,4,256,128]{2,3,0,1:T(8,128)(2,1)}, bf16[3,4,256,128]{2,3,0,1:T(8,128)(2,1)}, f32[3,12,256,128]{3,1,2,0:T(8,128)}, f32[3,12,2...) while((s32[]{:T(128)}, ...), condition=%wide.region_4.5_spmd, body=%wide.region_0.4_spmd.sunk | while | flops 1345845504 | bytes 75555744 | solution.py:105
  119.2 1.6 gather_fusion
  120.8 1.6 gather_fusion.1
  122.3 1.9 fusion.79
  124.9 2.0 fusion.81
  128.7 3.0 fusion.84
  131.8 2.0 multiply_reduce_fusion.2
  135.6 1.5 fusion.83
  138.0 1.7 constant_dynamic-update-slice_fusion.7
  139.7 4.0 %bitcast_dynamic-update-slice_fusion.4 = f32[3,12,256,128]{3,1,2,0:T(8,128)} fusion(f32[3,12,256,128]{3,1,2,0:T(8,128)} %get-tuple-element.228, s32[]{:T(128)S(6)} %copy.106, f32[4,3,256,128]{3,2,1,0:T(8,128)S(1)} %fusion.83, s32[4,3]{0,1:T(4,128)S(1)} %copy.96), kind=kOutput, calls=%fused_computation.10.clone.1 | convolution fusion | flops 56623248 | bytes 3670068 | tf_op jit(solution)/shard_map/while/body/eval_jaxpr/anj,ankd->jkd/dot_general | solution.py:71
  143.7 4.0 %bitcast_dynamic-update-slice_fusion.5 = f32[3,12,256,128]{3,1,2,0:T(8,128)} fusion(f32[3,12,256,128]{3,1,2,0:T(8,128)} %get-tuple-element.229, s32[]{:T(128)S(6)} %copy.106, f32[4,3,256,128]{3,2,1,0:T(8,128)S(1)} %copy-done.1, s32[4,3]{0,1:T(4,128)S(1)} %copy.96), kind=kOutput, calls=%fused_computation.9.clone.1 | convolution fusion | flops 56623248 | bytes 3670068 | tf_op jit(solution)/shard_map/while/body/eval_jaxpr/anj,ankd->jkd/dot_general | solution.py:72
  150.1 1.6 gather_fusion
  151.6 1.6 gather_fusion.1
  153.2 1.9 fusion.79
  155.8 2.0 fusion.81
  159.6 3.0 fusion.84
  162.6 2.0 multiply_reduce_fusion.2
  168.9 1.7 constant_dynamic-update-slice_fusion.7
  170.5 4.0 %bitcast_dynamic-update-slice_fusion.4 = f32[3,12,256,128]{3,1,2,0:T(8,128)} fusion(f32[3,12,256,128]{3,1,2,0:T(8,128)} %get-tuple-element.228, s32[]{:T(128)S(6)} %copy.106, f32[4,3,256,128]{3,2,1,0:T(8,128)S(1)} %fusion.83, s32[4,3]{0,1:T(4,128)S(1)} %copy.96), kind=kOutput, calls=%fused_computation.10.clone.1 | convolution fusion | flops 56623248 | bytes 3670068 | tf_op jit(solution)/shard_map/while/body/eval_jaxpr/anj,ankd->jkd/dot_general | solution.py:71
  174.5 4.0 %bitcast_dynamic-update-slice_fusion.5 = f32[3,12,256,128]{3,1,2,0:T(8,128)} fusion(f32[3,12,256,128]{3,1,2,0:T(8,128)} %get-tuple-element.229, s32[]{:T(128)S(6)} %copy.106, f32[4,3,256,128]{3,2,1,0:T(8,128)S(1)} %copy-done.1, s32[4,3]{0,1:T(4,128)S(1)} %copy.96), kind=kOutput, calls=%fused_computation.9.clone.1 | convolution fusion | flops 56623248 | bytes 3670068 | tf_op jit(solution)/shard_map/while/body/eval_jaxpr/anj,ankd->jkd/dot_general | solution.py:72
  180.9 1.6 gather_fusion
  182.4 1.6 gather_fusion.1
  184.0 1.9 fusion.79
  186.6 2.0 fusion.81
  190.4 3.0 fusion.84
  193.4 2.0 multiply_reduce_fusion.2
  197.3 1.5 fusion.83
  199.7 1.7 constant_dynamic-update-slice_fusion.7
  201.3 4.0 %bitcast_dynamic-update-slice_fusion.4 = f32[3,12,256,128]{3,1,2,0:T(8,128)} fusion(f32[3,12,256,128]{3,1,2,0:T(8,128)} %get-tuple-element.228, s32[]{:T(128)S(6)} %copy.106, f32[4,3,256,128]{3,2,1,0:T(8,128)S(1)} %fusion.83, s32[4,3]{0,1:T(4,128)S(1)} %copy.96), kind=kOutput, calls=%fused_computation.10.clone.1 | convolution fusion | flops 56623248 | bytes 3670068 | tf_op jit(solution)/shard_map/while/body/eval_jaxpr/anj,ankd->jkd/dot_general | solution.py:71
  205.4 4.0 %bitcast_dynamic-update-slice_fusion.5 = f32[3,12,256,128]{3,1,2,0:T(8,128)} fusion(f32[3,12,256,128]{3,1,2,0:T(8,128)} %get-tuple-element.229, s32[]{:T(128)S(6)} %copy.106, f32[4,3,256,128]{3,2,1,0:T(8,128)S(1)} %copy-done.1, s32[4,3]{0,1:T(4,128)S(1)} %copy.96), kind=kOutput, calls=%fused_computation.9.clone.1 | convolution fusion | flops 56623248 | bytes 3670068 | tf_op jit(solution)/shard_map/while/body/eval_jaxpr/anj,ankd->jkd/dot_general | solution.py:72
  209.4 6.8 %copy.58 = f32[12,256,3,128]{1,0,3,2:T(8,128)} copy(f32[12,256,3,128]{3,0,1,2:T(8,128)} %bitcast.173) | data formatting | bytes 9437184 | tf_op jit(solution)/shard_map/transpose | solution.py:42
  216.2 6.9 %stack_reshape.7 = f32[1,3072,384]{1,2,0:T(8,128)} reshape(f32[12,256,3,128]{1,0,3,2:T(8,128)} %copy.58) | data formatting | bytes 9437184 | tf_op jit(solution)/shard_map/stack;reshape | solution.py:108
  223.0 6.7 %copy.57 = f32[12,256,3,128]{1,0,3,2:T(8,128)} copy(f32[12,256,3,128]{3,0,1,2:T(8,128)} %bitcast.174) | data formatting | bytes 9437184 | tf_op jit(solution)/shard_map/transpose | solution.py:42
  229.7 6.9 %stack_reshape.6 = f32[1,3072,384]{1,2,0:T(8,128)} reshape(f32[12,256,3,128]{1,0,3,2:T(8,128)} %copy.57) | data formatting | bytes 9437184 | tf_op jit(solution)/shard_map/stack;reshape | solution.py:108
  236.5 2.8 constant_dynamic-update-slice_fusion.3
  241.4 2.9 copy-done.2
  245.8 2.6 collective-permute-start.2
  249.7 14.7 %all_to_all.134 = bf16[4,256,384]{1,2,0:T(8,128)(2,1)S(1)} all-to-all(bf16[4,256,384]{1,2,0:T(8,128)(2,1)S(1)} %bitcast.184), channel_id=1, replica_groups=mesh['groups'=2,'seq'=4,'head'=4] {'head'}, dimensions={0} | all-to-all | bytes 1572864 | tf_op jit(solution)/shard_map/all_to_all | solution.py:115
  264.4 3.5 %all-to-all-start.5 = ((bf16[4,256,384]{1,2,0:T(8,128)(2,1)}), bf16[4,256,384]{1,2,0:T(8,128)(2,1)S(1)}, u32[]{:S(2)}, u32[]{:S(2)}) async-start(bf16[4,256,384]{1,2,0:T(8,128)(2,1)} %bitcast.183), calls=%async_computation.5 | async-start | bytes 1572864 | tf_op jit(solution)/shard_map/all_to_all | solution.py:116
  267.9 14.0 %collective-permute-done.2 = bf16[2,1024,384]{1,2,0:T(8,128)(2,1)} collective-permute-done((bf16[2,1024,384]{1,2,0:T(8,128)(2,1)}, bf16[2,1024,384]{1,2,0:T(8,128)(2,1)}, u32[]{:S(2)}, u32[]{:S(2)}) %collective-permute-start.2) | collective-permute-done | bytes 1572896 | tf_op jit(solution)/shard_map/ppermute | solution.py:30
  281.9 5.1 %collective-permute-done.3 = bf16[2,1024,384]{1,2,0:T(8,128)(2,1)} collective-permute-done((bf16[2,1024,384]{1,2,0:T(8,128)(2,1)S(1)}, bf16[2,1024,384]{1,2,0:T(8,128)(2,1)}, u32[]{:S(2)}, u32[]{:S(2)}) %collective-permute-start.3) | collective-permute-done | bytes 1572896 | tf_op jit(solution)/shard_map/ppermute | solution.py:30
  287.0 3.7 %fusion.35 = bf16[2,1024,384]{1,2,0:T(8,128)(2,1)S(1)} fusion(f32[2,3072,384]{1,2,0:T(8,128)} %copy-done.2, bf16[2,1024,384]{1,2,0:T(8,128)(2,1)} %collective-permute-done.3, bf16[2,1024,384]{1,2,0:T(8,128)(2,1)} %collective-permute-done.2), kind=kLoop, calls=%fused_computation.50 | loop fusion | flops 3932160 | bytes 7864320 | tf_op jit(solution)/shard_map/convert.1
  292.0 3.5 %all-to-all-start.7 = ((bf16[4,256,384]{2,1,0:T(8,128)(2,1)}), bf16[4,256,384]{2,1,0:T(8,128)(2,1)S(1)}, u32[]{:S(2)}, u32[]{:S(2)}) async-start(bf16[4,256,384]{2,1,0:T(8,128)(2,1)} %bitcast.55), calls=%async_computation.7 | async-start | bytes 1572864 | tf_op jit(solution)/shard_map/all_to_all | solution.py:120
  296.6 10.5 %all-to-all-done.7 = bf16[4,256,384]{2,1,0:T(8,128)(2,1)S(1)} async-done(((bf16[4,256,384]{2,1,0:T(8,128)(2,1)}), bf16[4,256,384]{2,1,0:T(8,128)(2,1)S(1)}, u32[]{:S(2)}, u32[]{:S(2)}) %all-to-all-start.7) | async-done | bytes 786464 | tf_op jit(solution)/shard_map/all_to_all | solution.py:120
  307.1 3.5 %all-to-all-start.6 = ((bf16[4,256,384]{2,1,0:T(8,128)(2,1)}), bf16[4,256,384]{2,1,0:T(8,128)(2,1)S(1)}, u32[]{:S(2)}, u32[]{:S(2)}) async-start(bf16[4,256,384]{2,1,0:T(8,128)(2,1)} %bitcast.52), calls=%async_computation.6 | async-start | bytes 1572864 | tf_op jit(solution)/shard_map/all_to_all | solution.py:117
  314.3 7.9 %all-to-all-done.6 = bf16[4,256,384]{2,1,0:T(8,128)(2,1)S(1)} async-done(((bf16[4,256,384]{2,1,0:T(8,128)(2,1)}), bf16[4,256,384]{2,1,0:T(8,128)(2,1)S(1)}, u32[]{:S(2)}, u32[]{:S(2)}) %all-to-all-start.6) | async-done | bytes 786464 | tf_op jit(solution)/shard_map/all_to_all | solution.py:117
  (117 shorter events, 43.7 us)
Async XLA Ops:
  0.6 5.9 %copy-start.8 = (bf16[256,1536]{1,0:T(8,128)(2,1)S(1)}, bf16[256,1536]{1,0:T(8,128)(2,1)}, u32[]{:S(2)}) copy-start(bf16[256,1536]{1,0:T(8,128)(2,1)} %param.10) | copy-start | bytes 2359300
  3.0 15.1 %all-to-all-start.1 = ((bf16[256,4,384]{0,2,1:T(8,128)(2,1)}), bf16[256,4,384]{0,2,1:T(8,128)(2,1)S(1)}, u32[]{:S(2)}, u32[]{:S(2)}) async-start(bf16[256,4,384]{0,2,1:T(8,128)(2,1)} %bitcast.30), calls=%async_computation.1 | async-start | bytes 1572864 | tf_op jit(solution)/shard_map/all_to_all | solution.py:82
  18.1 15.1 %all-to-all-start.2 = ((bf16[256,4,384]{0,2,1:T(8,128)(2,1)}), bf16[256,4,384]{0,2,1:T(8,128)(2,1)S(1)}, u32[]{:S(2)}, u32[]{:S(2)}) async-start(bf16[256,4,384]{0,2,1:T(8,128)(2,1)} %bitcast.33), calls=%async_computation.2 | async-start | bytes 1572864 | tf_op jit(solution)/shard_map/all_to_all | solution.py:83
  22.0 17.8 %copy-start.9 = (bf16[256,1536]{1,0:T(8,128)(2,1)S(1)}, bf16[256,1536]{1,0:T(8,128)(2,1)}, u32[]{:S(2)}) copy-start(bf16[256,1536]{1,0:T(8,128)(2,1)} %param.8) | copy-start | bytes 2359300
  33.6 10.9 %copy-start.12 = (s32[16,3]{0,1:T(4,128)S(1)}, s32[16,3]{0,1:T(4,128)}, u32[]{:S(2)}) copy-start(s32[16,3]{0,1:T(4,128)} %param.12) | copy-start | bytes 580
  33.6 10.9 %copy-start.13 = (s32[16,3]{0,1:T(4,128)S(1)}, s32[16,3]{0,1:T(4,128)}, u32[]{:S(2)}) copy-start(s32[16,3]{0,1:T(4,128)} %param.13) | copy-start | bytes 580
  33.6 11.1 %copy-start.10 = (bf16[256,1536]{1,0:T(8,128)(2,1)S(1)}, bf16[256,1536]{1,0:T(8,128)(2,1)}, u32[]{:S(2)}) copy-start(bf16[256,1536]{1,0:T(8,128)(2,1)} %param.11) | copy-start | bytes 2359300
  35.0 36.1 %collective-permute-start.1 = (bf16[2,1024,384]{2,1,0:T(8,128)(2,1)}, bf16[2,1024,384]{2,1,0:T(8,128)(2,1)}, u32[]{:S(2)}, u32[]{:S(2)}) collective-permute-start(bf16[2,1024,384]{2,1,0:T(8,128)(2,1)} %pad_maximum_fusion.1), channel_id=1, source_target_pairs={{4,0},{8,4},{12,8},{5,1},{9,5},{13,9},{6,2},{10,6},{14,10},{7,3},{... | collective-permute-start | bytes 4718600 | tf_op jit(solution)/shard_map/ppermute | solution.py:20
  38.5 37.9 %collective-permute-start = (bf16[2,1024,384]{2,1,0:T(8,128)(2,1)}, bf16[2,1024,384]{2,1,0:T(8,128)(2,1)}, u32[]{:S(2)}, u32[]{:S(2)}) collective-permute-start(bf16[2,1024,384]{2,1,0:T(8,128)(2,1)} %pad_maximum_fusion.1), channel_id=1, source_target_pairs={{0,4},{4,8},{8,12},{1,5},{5,9},{9,13},{2,6},{6,10},{10,14},{3,7},{... | collective-permute-start | bytes 4718600 | tf_op jit(solution)/shard_map/ppermute | solution.py:18
  40.9 40.1 %all-to-all-start = ((bf16[256,4,384]{0,2,1:T(8,128)(2,1)}), bf16[256,4,384]{0,2,1:T(8,128)(2,1)S(1)}, u32[]{:S(2)}, u32[]{:S(2)}) async-start(bf16[256,4,384]{0,2,1:T(8,128)(2,1)} %bitcast.26), calls=%async_computation | async-start | bytes 1572864 | tf_op jit(solution)/shard_map/all_to_all | solution.py:81
  81.0 35.9 %all-to-all-start.3 = ((bf16[256,4,384]{0,2,1:T(8,128)(2,1)}), bf16[256,4,384]{0,2,1:T(8,128)(2,1)}, u32[]{:S(2)}, u32[]{:S(2)}) async-start(bf16[256,4,384]{0,2,1:T(8,128)(2,1)} %bitcast.38), calls=%async_computation.3 | async-start | bytes 1572864 | tf_op jit(solution)/shard_map/all_to_all | solution.py:84
  116.8 0.9 copy-start.6
  122.3 2.6 copy-start.3
  128.7 3.0 copy-start.4
  133.7 1.1 copy-start
  137.1 6.5 %copy-start.1 = (f32[4,3,256,128]{3,2,1,0:T(8,128)S(1)}, f32[4,3,256,128]{3,2,1,0:T(8,128)}, u32[]{:S(2)}) copy-start(f32[4,3,256,128]{3,2,1,0:T(8,128)} %fusion.84) | copy-start | bytes 4718596 | tf_op jit(solution)/shard_map/while
  143.7 4.0 %copy-start.7 = (bf16[3,4,256,128]{2,3,0,1:T(8,128)(2,1)S(1)}, bf16[3,4,256,128]{2,3,0,1:T(8,128)(2,1)}, u32[]{:S(2)}) copy-start(bf16[3,4,256,128]{2,3,0,1:T(8,128)(2,1)} %copy-done.6) | copy-start | bytes 2359300 | tf_op jit(solution)/shard_map/while
  147.7 0.9 copy-start.6
  153.2 2.6 copy-start.3
  159.6 3.0 copy-start.4
  164.6 1.1 copy-start
  168.0 6.5 %copy-start.1 = (f32[4,3,256,128]{3,2,1,0:T(8,128)S(1)}, f32[4,3,256,128]{3,2,1,0:T(8,128)}, u32[]{:S(2)}) copy-start(f32[4,3,256,128]{3,2,1,0:T(8,128)} %fusion.84) | copy-start | bytes 4718596 | tf_op jit(solution)/shard_map/while
  174.5 4.0 %copy-start.7 = (bf16[3,4,256,128]{2,3,0,1:T(8,128)(2,1)S(1)}, bf16[3,4,256,128]{2,3,0,1:T(8,128)(2,1)}, u32[]{:S(2)}) copy-start(bf16[3,4,256,128]{2,3,0,1:T(8,128)(2,1)} %copy-done.6) | copy-start | bytes 2359300 | tf_op jit(solution)/shard_map/while
  178.5 0.9 copy-start.6
  184.0 2.6 copy-start.3
  190.4 3.0 copy-start.4
  195.4 1.1 copy-start
  198.8 6.6 %copy-start.1 = (f32[4,3,256,128]{3,2,1,0:T(8,128)S(1)}, f32[4,3,256,128]{3,2,1,0:T(8,128)}, u32[]{:S(2)}) copy-start(f32[4,3,256,128]{3,2,1,0:T(8,128)} %fusion.84) | copy-start | bytes 4718596 | tf_op jit(solution)/shard_map/while
  205.4 4.0 %copy-start.7 = (bf16[3,4,256,128]{2,3,0,1:T(8,128)(2,1)S(1)}, bf16[3,4,256,128]{2,3,0,1:T(8,128)(2,1)}, u32[]{:S(2)}) copy-start(bf16[3,4,256,128]{2,3,0,1:T(8,128)(2,1)} %copy-done.6) | copy-start | bytes 2359300 | tf_op jit(solution)/shard_map/while
  236.5 3.8 %copy-start.5 = (f32[1,3072,384]{1,2,0:T(8,128)S(1)}, f32[1,3072,384]{1,2,0:T(8,128)}, u32[]{:S(2)}) copy-start(f32[1,3072,384]{1,2,0:T(8,128)} %stack_reshape.7) | copy-start | bytes 14155780
  240.6 3.7 %copy-start.2 = (f32[2,3072,384]{1,2,0:T(8,128)}, f32[2,3072,384]{1,2,0:T(8,128)S(1)}, u32[]{:S(2)}) copy-start(f32[2,3072,384]{1,2,0:T(8,128)S(1)} %constant_dynamic-update-slice_fusion.2) | copy-start | bytes 28311556
  244.3 5.4 %copy-start.11 = (bf16[3,4,256,128]{2,3,0,1:T(8,128)(2,1)S(1)}, bf16[3,4,256,128]{2,3,0,1:T(8,128)(2,1)}, u32[]{:S(2)}) copy-start(bf16[3,4,256,128]{2,3,0,1:T(8,128)(2,1)} %get-tuple-element.64) | copy-start | bytes 2359300
  245.8 36.1 %collective-permute-start.2 = (bf16[2,1024,384]{1,2,0:T(8,128)(2,1)}, bf16[2,1024,384]{1,2,0:T(8,128)(2,1)}, u32[]{:S(2)}, u32[]{:S(2)}) collective-permute-start(bf16[2,1024,384]{1,2,0:T(8,128)(2,1)} %get-tuple-element.126), channel_id=1, source_target_pairs={{4,0},{8,4},{12,8},{5,1},{9,5},{13,9},{6,2},{10,6},{14,10},{7,3},{... | collective-permute-start | bytes 4718600 | tf_op jit(solution)/shard_map/ppermute | solution.py:30
  248.4 38.6 %collective-permute-start.3 = (bf16[2,1024,384]{1,2,0:T(8,128)(2,1)S(1)}, bf16[2,1024,384]{1,2,0:T(8,128)(2,1)}, u32[]{:S(2)}, u32[]{:S(2)}) collective-permute-start(bf16[2,1024,384]{1,2,0:T(8,128)(2,1)S(1)} %get-tuple-element.127), channel_id=1, source_target_pairs={{0,4},{4,8},{8,12},{1,5},{5,9},{9,13},{2,6},{6,10},{10,14},{3,7},{... | collective-permute-start | bytes 4718600 | tf_op jit(solution)/shard_map/ppermute | solution.py:30
  264.4 27.6 %all-to-all-start.5 = ((bf16[4,256,384]{1,2,0:T(8,128)(2,1)}), bf16[4,256,384]{1,2,0:T(8,128)(2,1)S(1)}, u32[]{:S(2)}, u32[]{:S(2)}) async-start(bf16[4,256,384]{1,2,0:T(8,128)(2,1)} %bitcast.183), calls=%async_computation.5 | async-start | bytes 1572864 | tf_op jit(solution)/shard_map/all_to_all | solution.py:116
  292.0 15.1 %all-to-all-start.7 = ((bf16[4,256,384]{2,1,0:T(8,128)(2,1)}), bf16[4,256,384]{2,1,0:T(8,128)(2,1)S(1)}, u32[]{:S(2)}, u32[]{:S(2)}) async-start(bf16[4,256,384]{2,1,0:T(8,128)(2,1)} %bitcast.55), calls=%async_computation.7 | async-start | bytes 1572864 | tf_op jit(solution)/shard_map/all_to_all | solution.py:120
  307.1 15.1 %all-to-all-start.6 = ((bf16[4,256,384]{2,1,0:T(8,128)(2,1)}), bf16[4,256,384]{2,1,0:T(8,128)(2,1)S(1)}, u32[]{:S(2)}, u32[]{:S(2)}) async-start(bf16[4,256,384]{2,1,0:T(8,128)(2,1)} %bitcast.52), calls=%async_computation.6 | async-start | bytes 1572864 | tf_op jit(solution)/shard_map/all_to_all | solution.py:117
where the time goes:
time: 326 us; the launch traced here: 324 us
  local copies, waits for them, and re-layouts  111 us (34%)
  waiting for transfers between devices  89.5 us (27%)
  matrix products  57.4 us (18%)
  starting transfers between devices  33.8 us (10%)
  other arithmetic  15.9 us (5%)
  blocking collectives  14.7 us (5%)
    ppermute x1, waiting for transfers between devices, extended_2(): lax.ppermute(head, axis, [((i + 1) % count, i) for i in range(ends)])  25.2 us
    ppermute x2, waiting for transfers between devices, shifted(): lax.ppermute(value, axis, [(source, source + steps) for source in range(i...  19.1 us
    unnamed x27, local copies, waits for them, and re-layouts  17.3 us
    all_to_all x1, blocking collectives, body(): lax.all_to_all(head_join(attended), 'head', split_axis=0, concat_axis=1,...  14.7 us
    another operation x3, local copies, waits for them, and re-layouts, body(): grads = jnp.stack([head_join(key_sums), head_join(value_sums)])  14 us
    transpose x2, local copies, waits for them, and re-layouts, head_join(): blocks.transpose(1, 2, 0, 3).reshape(tiles * tile_size, heads * head_size)  13.5 us
    dynamic_update_slice x12, local copies, waits for them, and re-layouts, body(): lax.map(with_partials, (q_heads, g_heads, k_heads, v_heads))  13 us
    dot_general x3, matrix products, forward_head(): jnp.einsum('anj,ankd->jkd', onehot, value_slots, precision=lax.Precision....  12.1 us
  transfers between devices with their start and end apart: 11, of which 8 were waited for; matrix products, arithmetic and copies ran while one was open for 16% of the time, Pallas kernels for 0%

commit v1 on v0

--- a/solution.py
+++ b/solution.py
@@ -5,6 +5,19 @@
 
 HEADS = 12
 HEAD_DIM = 128
+
+
+def build_domain(payload, d0, local):
+    reply, back = (payload.shape[:d0], payload.shape[d0 + 1 :])
+    tmp = jnp.moveaxis(payload.reshape(*reply, local, -1, *back), d0, 0)
+    return tmp
+
+
+def extend_tails(buf, dim_k):
+    aux = list(buf.shape[1:])
+    aux[dim_k] *= buf.shape[0]
+    piece_now = jnp.moveaxis(buf, 0, dim_k).reshape(aux)
+    return piece_now
 
 
 def extended_2(cells, sides, width):
@@ -111,8 +124,25 @@
     owned = grads[:, margin : 2 * margin] + from_above + from_below
     key_own = owned[0]
     value_own = owned[1]
+
+    def reach_the_trails(sheet, named_axis, mat, local_x):
+        val2, everything = (lax.axis_size(named_axis), lax.axis_index(named_axis))
+        step_out = build_domain(sheet, mat, val2)
+        arr_next = step_out
+        u = 1
+        while u < val2:
+            now, raw_out = ((everything + u) % val2, (everything - u) % val2)
+            base_arr = lax.dynamic_index_in_dim(step_out, now, 0)
+            outcome_arr = lax.ppermute(
+                base_arr, axis_name=named_axis, perm=[(pp, (pp + u) % val2) for pp in range(val2)]
+            )
+            arr_next = lax.dynamic_update_slice_in_dim(arr_next, outcome_arr, raw_out, axis=0)
+            u = u + 1
+        clean = extend_tails(arr_next, local_x)
+        return clean
+
     result = (
-        lax.all_to_all(head_join(attended), "head", split_axis=0, concat_axis=1, tiled=True),
+        reach_the_trails(head_join(attended), "head", 0, 1),
         lax.all_to_all(head_join(query_grad), "head", split_axis=0, concat_axis=1, tiled=True),
         lax.all_to_all(
             key_own.astype(jnp.bfloat16), "head", split_axis=0, concat_axis=1, tiled=True

time: 326 us -> 355 us (1.089); the launches traced: 324 us -> 349 us
  waiting for transfers between devices: 89.5 us -> 105 us
  blocking collectives: 14.7 us -> 0 us
  local copies, waits for them, and re-layouts: 111 us -> 120 us
  matrix products: 57.4 us -> 63.6 us
  starting transfers between devices: 33.8 us -> 39.3 us
  other arithmetic: 15.9 us -> 19.6 us
    all_to_all x1 -> x0, blocking collectives: 14.7 us -> none  [body(): lax.all_to_all(head_join(attended), 'head', split_axis=0, concat_axis=1,...]
    ppermute x0 -> x3, waiting for transfers between devices: none -> 13.2 us  [reach_the_trails(): lax.ppermute(base_arr, axis_name=named_axis, perm=[(pp, (pp + u) % val2)...]
    all_to_all x1, waiting for transfers between devices: 10.5 us -> 0.01 us  [body(): lax.all_to_all(value_own.astype(jnp.bfloat16), 'head', split_axis=0, conc...]
    ppermute x2, waiting for transfers between devices: 19.1 us -> 29.3 us  [shifted(): lax.ppermute(value, axis, [(source, source + steps) for source in range(i...]
    dot_general x3, matrix products: 4.59 us -> 9.4 us  [forward_head(): jnp.einsum('aqnk,aqd->ankd', score_grad, q_tile, preferred_element_type=j...]
    another operation x3, local copies, waits for them, and re-layouts: 14 us -> 18.8 us  [body(): grads = jnp.stack([head_join(key_sums), head_join(value_sums)])]
    dot_general x3, matrix products: 12 us -> 16.2 us  [forward_head(): jnp.einsum('anj,ankd->jkd', onehot, key_slots, precision=lax.Precision.HI...]
    while x36 -> x30, local copies, waits for them, and re-layouts: 2.2 us -> 6.24 us
  transfers between devices with their start and end apart: 11 -> 14, of which waited for: 8 -> 8; matrix products, arithmetic and copies ran while one was open for 16% -> 15% of each run, Pallas kernels for 0% -> 0%
where the time goes in v1:
time: 355 us; the launch traced here: 349 us
  local copies, waits for them, and re-layouts  120 us (34%)
  waiting for transfers between devices  105 us (30%)
  matrix products  63.6 us (18%)
  starting transfers between devices  39.3 us (11%)
  other arithmetic  19.6 us (6%)
    ppermute x2, waiting for transfers between devices, shifted(): lax.ppermute(value, axis, [(source, source + steps) for source in range(i...  29.3 us
    ppermute x1, waiting for transfers between devices, extended_2(): lax.ppermute(head, axis, [((i + 1) % count, i) for i in range(ends)])  25.2 us
    another operation x3, local copies, waits for them, and re-layouts, body(): grads = jnp.stack([head_join(key_sums), head_join(value_sums)])  18.8 us
    dot_general x3, matrix products, forward_head(): jnp.einsum('anj,ankd->jkd', onehot, key_slots, precision=lax.Precision.HI...  16.2 us
    unnamed x23, local copies, waits for them, and re-layouts  15.8 us
    transpose x2, local copies, waits for them, and re-layouts, head_join(): blocks.transpose(1, 2, 0, 3).reshape(tiles * tile_size, heads * head_size)  13.5 us
    ppermute x3, waiting for transfers between devices, reach_the_trails(): lax.ppermute(base_arr, axis_name=named_axis, perm=[(pp, (pp + u) % val2)...  13.2 us
    dynamic_update_slice x12, local copies, waits for them, and re-layouts, body(): lax.map(with_partials, (q_heads, g_heads, k_heads, v_heads))  13 us
  transfers between devices with their start and end apart: 14, of which 8 were waited for; matrix products, arithmetic and copies ran while one was open for 15% of the time, Pallas kernels for 0%

profile of v1, /device:TPU:24, one launch (start us, length us, event | category | flops | bytes accessed | tf_op | source)
XLA Modules:
  0.0 348.8 jit_solution(17161123764638569950)
XLA Ops:
  0.6 2.4 copy.45
  3.0 3.5 %all-to-all-start.2 = ((bf16[256,4,384]{0,2,1:T(8,128)(2,1)}), bf16[256,4,384]{0,2,1:T(8,128)(2,1)S(1)}, u32[]{:S(2)}, u32[]{:S(2)}) async-start(bf16[256,4,384]{0,2,1:T(8,128)(2,1)} %bitcast.33), calls=%async_computation.2 | async-start | bytes 1572864 | tf_op jit(solution)/shard_map/all_to_all | solution.py:96
  7.7 10.5 %all-to-all-done.2 = bf16[256,4,384]{0,2,1:T(8,128)(2,1)S(1)} async-done(((bf16[256,4,384]{0,2,1:T(8,128)(2,1)}), bf16[256,4,384]{0,2,1:T(8,128)(2,1)S(1)}, u32[]{:S(2)}, u32[]{:S(2)}) %all-to-all-start.2) | async-done | bytes 786464 | tf_op jit(solution)/shard_map/all_to_all | solution.py:96
  18.1 3.5 %all-to-all-start.1 = ((bf16[256,4,384]{0,2,1:T(8,128)(2,1)}), bf16[256,4,384]{0,2,1:T(8,128)(2,1)S(1)}, u32[]{:S(2)}, u32[]{:S(2)}) async-start(bf16[256,4,384]{0,2,1:T(8,128)(2,1)} %bitcast.30), calls=%async_computation.1 | async-start | bytes 1572864 | tf_op jit(solution)/shard_map/all_to_all | solution.py:95
  22.0 11.2 %all-to-all-done.1 = bf16[256,4,384]{0,2,1:T(8,128)(2,1)S(1)} async-done(((bf16[256,4,384]{0,2,1:T(8,128)(2,1)}), bf16[256,4,384]{0,2,1:T(8,128)(2,1)S(1)}, u32[]{:S(2)}, u32[]{:S(2)}) %all-to-all-start.1) | async-done | bytes 786464 | tf_op jit(solution)/shard_map/all_to_all | solution.py:95
  35.0 3.5 %collective-permute-start.1 = (bf16[2,1024,384]{2,1,0:T(8,128)(2,1)}, bf16[2,1024,384]{2,1,0:T(8,128)(2,1)}, u32[]{:S(2)}, u32[]{:S(2)}) collective-permute-start(bf16[2,1024,384]{2,1,0:T(8,128)(2,1)} %pad_maximum_fusion.1), channel_id=1, source_target_pairs={{4,0},{8,4},{12,8},{5,1},{9,5},{13,9},{6,2},{10,6},{14,10},{7,3},{... | collective-permute-start | bytes 4718600 | tf_op jit(solution)/shard_map/ppermute | solution.py:33
  40.9 3.5 %all-to-all-start = ((bf16[256,4,384]{0,2,1:T(8,128)(2,1)}), bf16[256,4,384]{0,2,1:T(8,128)(2,1)S(1)}, u32[]{:S(2)}, u32[]{:S(2)}) async-start(bf16[256,4,384]{0,2,1:T(8,128)(2,1)} %bitcast.26), calls=%async_computation | async-start | bytes 1572864 | tf_op jit(solution)/shard_map/all_to_all | solution.py:94
  45.9 25.2 %collective-permute-done.1 = bf16[2,1024,384]{2,1,0:T(8,128)(2,1)} collective-permute-done((bf16[2,1024,384]{2,1,0:T(8,128)(2,1)}, bf16[2,1024,384]{2,1,0:T(8,128)(2,1)}, u32[]{:S(2)}, u32[]{:S(2)}) %collective-permute-start.1) | collective-permute-done | bytes 1572896 | tf_op jit(solution)/shard_map/ppermute | solution.py:33
  71.1 5.2 %collective-permute-done = bf16[2,1024,384]{2,1,0:T(8,128)(2,1)} collective-permute-done((bf16[2,1024,384]{2,1,0:T(8,128)(2,1)}, bf16[2,1024,384]{2,1,0:T(8,128)(2,1)}, u32[]{:S(2)}, u32[]{:S(2)}) %collective-permute-start) | collective-permute-done | bytes 1572896 | tf_op jit(solution)/shard_map/ppermute | solution.py:31
  76.3 4.7 %pad_maximum_fusion = bf16[2,3072,384]{2,1,0:T(8,128)(2,1)} fusion(bf16[2,1024,384]{2,1,0:T(8,128)(2,1)} %collective-permute-done.1, bf16[1,1024,384]{2,1,0:T(8,128)(2,1)S(1)} %bitcast.170, bf16[1,1024,384]{2,1,0:T(8,128)(2,1)S(1)} %bitcast.172, bf16[2,1024,384]{2,1,0:T(8,128)(2,1)} %collective-permute-done), kind=kLoop, calls=%fused_computation.47 | loop fusion | flops 18874368 | bytes 9437184 | tf_op jit(solution)/shard_map/concatenate | solution.py:29
  81.0 4.2 %all-to-all-start.3 = ((bf16[256,4,384]{0,2,1:T(8,128)(2,1)}), bf16[256,4,384]{0,2,1:T(8,128)(2,1)}, u32[]{:S(2)}, u32[]{:S(2)}) async-start(bf16[256,4,384]{0,2,1:T(8,128)(2,1)} %bitcast.38), calls=%async_computation.3 | async-start | bytes 1572864 | tf_op jit(solution)/shard_map/all_to_all | solution.py:97
  85.2 4.3 %fusion.37 = (bf16[1,3072,384]{2,1,0:T(8,128)(2,1)S(1)}, bf16[1,3072,384]{2,1,0:T(8,128)(2,1)}) fusion(bf16[2,3072,384]{2,1,0:T(8,128)(2,1)} %pad_maximum_fusion), kind=kLoop, calls=%fused_computation.65 | loop fusion | bytes 9437184 | tf_op jit(solution)/shard_map/slice | solution.py:111
  89.5 4.3 %copy.47 = bf16[1,3072,384]{1,2,0:T(8,128)(2,1)} copy(bf16[1,3072,384]{2,1,0:T(8,128)(2,1)} %get-tuple-element.129) | data formatting | bytes 4718592 | tf_op jit(solution)/shard_map/slice | solution.py:110
  93.7 5.4 %reshape_squeeze.6 = bf16[12,256,3,128]{1,0,3,2:T(8,128)(2,1)} reshape(bf16[1,3072,384]{1,2,0:T(8,128)(2,1)} %copy.47) | data formatting | bytes 4718592 | tf_op jit(solution)/shard_map/reshape;squeeze | solution.py:48
  99.1 4.8 %copy.52 = bf16[3,12,256,128]{3,2,1,0:T(8,128)(2,1)} copy(bf16[3,12,256,128]{2,1,3,0:T(8,128)(2,1)} %bitcast.167) | data formatting | bytes 4718592 | tf_op jit(solution)/shard_map/while | solution.py:118
  103.9 2.7 copy.49
  106.6 5.4 %reshape_squeeze.7 = bf16[12,256,3,128]{1,0,3,2:T(8,128)(2,1)} reshape(bf16[1,3072,384]{1,2,0:T(8,128)(2,1)} %copy.49) | data formatting | bytes 4718592 | tf_op jit(solution)/shard_map/reshape;squeeze | solution.py:48
  112.0 4.8 %copy.53 = bf16[3,12,256,128]{3,2,1,0:T(8,128)(2,1)} copy(bf16[3,12,256,128]{2,1,3,0:T(8,128)(2,1)} %bitcast.168) | data formatting | bytes 4718592 | tf_op jit(solution)/shard_map/while | solution.py:118
  116.8 102.8 %while.16 = (s32[]{:T(128)}, bf16[3,4,256,128]{2,3,0,1:T(8,128)(2,1)}, bf16[3,4,256,128]{2,3,0,1:T(8,128)(2,1)}, f32[3,12,256,128]{3,1,2,0:T(8,128)}, f32[3,12,2...) while((s32[]{:T(128)}, ...), condition=%wide.region_4.5_spmd, body=%wide.region_0.4_spmd.sunk | while | flops 1345845504 | bytes 72409984 | solution.py:118
  119.2 1.6 gather_fusion
  120.8 1.6 gather_fusion.1
  122.3 1.9 fusion.79
  124.9 2.0 fusion.81
  128.7 2.2 multiply_reduce_fusion.2
  134.8 1.7 constant_dynamic-update-slice_fusion.10
  136.5 3.1 fusion.83
  139.7 5.4 %bitcast_dynamic-update-slice_fusion.4 = f32[3,12,256,128]{3,1,2,0:T(8,128)} fusion(f32[3,12,256,128]{3,1,2,0:T(8,128)} %get-tuple-element.231, s32[]{:T(128)S(6)} %copy.106, f32[4,3,256,128]{3,2,1,0:T(8,128)} %fusion.83, s32[4,3]{0,1:T(4,128)S(1)} %copy.96), kind=kOutput, calls=%fused_computation.10.clone.1 | convolution fusion | flops 56623248 | bytes 3670068 | tf_op jit(solution)/shard_map/while/body/eval_jaxpr/anj,ankd->jkd/dot_general | solution.py:84
  145.2 1.8 fusion.84
  147.0 4.0 %bitcast_dynamic-update-slice_fusion.5 = f32[3,12,256,128]{3,1,2,0:T(8,128)} fusion(f32[3,12,256,128]{3,1,2,0:T(8,128)} %get-tuple-element.232, s32[]{:T(128)S(6)} %copy.106, f32[4,3,256,128]{3,2,1,0:T(8,128)S(1)} %fusion.84, s32[4,3]{0,1:T(4,128)S(1)} %copy.96), kind=kOutput, calls=%fused_computation.9.clone.1 | convolution fusion | flops 56623248 | bytes 3670068 | tf_op jit(solution)/shard_map/while/body/eval_jaxpr/anj,ankd->jkd/dot_general | solution.py:85
  153.5 1.6 gather_fusion
  155.1 1.6 gather_fusion.1
  156.6 1.9 fusion.79
  159.2 2.0 fusion.81
  163.0 2.2 multiply_reduce_fusion.2
  169.1 1.7 constant_dynamic-update-slice_fusion.10
  170.8 3.1 fusion.83
  174.0 5.4 %bitcast_dynamic-update-slice_fusion.4 = f32[3,12,256,128]{3,1,2,0:T(8,128)} fusion(f32[3,12,256,128]{3,1,2,0:T(8,128)} %get-tuple-element.231, s32[]{:T(128)S(6)} %copy.106, f32[4,3,256,128]{3,2,1,0:T(8,128)} %fusion.83, s32[4,3]{0,1:T(4,128)S(1)} %copy.96), kind=kOutput, calls=%fused_computation.10.clone.1 | convolution fusion | flops 56623248 | bytes 3670068 | tf_op jit(solution)/shard_map/while/body/eval_jaxpr/anj,ankd->jkd/dot_general | solution.py:84
  179.4 1.8 fusion.84
  181.3 4.0 %bitcast_dynamic-update-slice_fusion.5 = f32[3,12,256,128]{3,1,2,0:T(8,128)} fusion(f32[3,12,256,128]{3,1,2,0:T(8,128)} %get-tuple-element.232, s32[]{:T(128)S(6)} %copy.106, f32[4,3,256,128]{3,2,1,0:T(8,128)S(1)} %fusion.84, s32[4,3]{0,1:T(4,128)S(1)} %copy.96), kind=kOutput, calls=%fused_computation.9.clone.1 | convolution fusion | flops 56623248 | bytes 3670068 | tf_op jit(solution)/shard_map/while/body/eval_jaxpr/anj,ankd->jkd/dot_general | solution.py:85
  187.7 1.6 gather_fusion
  190.9 1.9 fusion.79
  193.4 2.0 fusion.81
  197.2 2.2 multiply_reduce_fusion.2
  203.4 1.7 constant_dynamic-update-slice_fusion.10
  205.0 3.1 fusion.83
  208.3 5.4 %bitcast_dynamic-update-slice_fusion.4 = f32[3,12,256,128]{3,1,2,0:T(8,128)} fusion(f32[3,12,256,128]{3,1,2,0:T(8,128)} %get-tuple-element.231, s32[]{:T(128)S(6)} %copy.106, f32[4,3,256,128]{3,2,1,0:T(8,128)} %fusion.83, s32[4,3]{0,1:T(4,128)S(1)} %copy.96), kind=kOutput, calls=%fused_computation.10.clone.1 | convolution fusion | flops 56623248 | bytes 3670068 | tf_op jit(solution)/shard_map/while/body/eval_jaxpr/anj,ankd->jkd/dot_general | solution.py:84
  213.7 1.8 fusion.84
  215.5 4.1 %bitcast_dynamic-update-slice_fusion.5 = f32[3,12,256,128]{3,1,2,0:T(8,128)} fusion(f32[3,12,256,128]{3,1,2,0:T(8,128)} %get-tuple-element.232, s32[]{:T(128)S(6)} %copy.106, f32[4,3,256,128]{3,2,1,0:T(8,128)S(1)} %fusion.84, s32[4,3]{0,1:T(4,128)S(1)} %copy.96), kind=kOutput, calls=%fused_computation.9.clone.1 | convolution fusion | flops 56623248 | bytes 3670068 | tf_op jit(solution)/shard_map/while/body/eval_jaxpr/anj,ankd->jkd/dot_general | solution.py:85
  219.6 6.8 %copy.57 = f32[12,256,3,128]{1,0,3,2:T(8,128)} copy(f32[12,256,3,128]{3,0,1,2:T(8,128)} %bitcast.173) | data formatting | bytes 9437184 | tf_op jit(solution)/shard_map/transpose | solution.py:55
  226.3 6.9 %stack_reshape.6 = f32[1,3072,384]{1,2,0:T(8,128)} reshape(f32[12,256,3,128]{1,0,3,2:T(8,128)} %copy.57) | data formatting | bytes 9437184 | tf_op jit(solution)/shard_map/stack;reshape | solution.py:121
  233.2 5.1 %constant_dynamic-update-slice_fusion.3 = f32[2,3072,384]{1,2,0:T(8,128)} fusion(f32[1,3072,384]{1,2,0:T(8,128)} %stack_reshape.6), kind=kLoop, calls=%fused_computation.53 | loop fusion | bytes 9437184
  238.3 6.7 %copy.58 = f32[12,256,3,128]{1,0,3,2:T(8,128)} copy(f32[12,256,3,128]{3,0,1,2:T(8,128)} %bitcast.174) | data formatting | bytes 9437184 | tf_op jit(solution)/shard_map/transpose | solution.py:55
  245.1 6.9 %stack_reshape.7 = f32[1,3072,384]{1,2,0:T(8,128)} reshape(f32[12,256,3,128]{1,0,3,2:T(8,128)} %copy.58) | data formatting | bytes 9437184 | tf_op jit(solution)/shard_map/stack;reshape | solution.py:121
  251.9 5.0 %constant_dynamic-update-slice_fusion.2 = f32[2,3072,384]{1,2,0:T(8,128)} fusion(f32[2,3072,384]{1,2,0:T(8,128)} %constant_dynamic-update-slice_fusion.3, f32[1,3072,384]{1,2,0:T(8,128)} %stack_reshape.7), kind=kLoop, calls=%fused_computation.52 | loop fusion | bytes 9437184 | tf_op jit(solution)/shard_map/stack | solution.py:121
  257.0 4.4 %convert.8 = bf16[2,3072,384]{1,2,0:T(8,128)(2,1)S(1)} convert(f32[2,3072,384]{1,2,0:T(8,128)} %constant_dynamic-update-slice_fusion.2) | non-fusion elementwise | flops 2359296 | bytes 14155776 | tf_op jit(solution)/shard_map/convert.3
  264.1 5.7 %collective-permute-start.5 = (bf16[2,1024,384]{1,2,0:T(8,128)(2,1)S(1)}, bf16[2,1024,384]{1,2,0:T(8,128)(2,1)}, u32[]{:S(2)}, u32[]{:S(2)}) collective-permute-start(bf16[2,1024,384]{1,2,0:T(8,128)(2,1)S(1)} %get-tuple-element.126), channel_id=1, source_target_pairs={{4,0},{8,4},{12,8},{5,1},{9,5},{13,9},{6,2},{10,6},{14,10},{7,3},{... | collective-permute-start | bytes 4718600 | tf_op jit(solution)/shard_map/ppermute | solution.py:43
  269.8 3.5 %all-to-all-start.4 = ((bf16[4,256,384]{1,2,0:T(8,128)(2,1)}), bf16[4,256,384]{1,2,0:T(8,128)(2,1)S(1)}, u32[]{:S(2)}, u32[]{:S(2)}) async-start(bf16[4,256,384]{1,2,0:T(8,128)(2,1)} %bitcast.48), calls=%async_computation.4 | async-start | bytes 1572864 | tf_op jit(solution)/shard_map/all_to_all | solution.py:146
  273.3 28.5 %collective-permute-done.6 = bf16[2,1024,384]{1,2,0:T(8,128)(2,1)} collective-permute-done((bf16[2,1024,384]{1,2,0:T(8,128)(2,1)}, bf16[2,1024,384]{1,2,0:T(8,128)(2,1)}, u32[]{:S(2)}, u32[]{:S(2)}) %collective-permute-start.6) | collective-permute-done | bytes 1572896 | tf_op jit(solution)/shard_map/ppermute | solution.py:43
  302.6 3.7 %fusion.35 = bf16[2,1024,384]{1,2,0:T(8,128)(2,1)S(1)} fusion(f32[2,3072,384]{1,2,0:T(8,128)} %constant_dynamic-update-slice_fusion.2, bf16[2,1024,384]{1,2,0:T(8,128)(2,1)} %collective-permute-done.6, bf16[2,1024,384]{1,2,0:T(8,128)(2,1)} %collective-permute-done.5), kind=kLoop, calls=%fused_computation.50 | loop fusion | flops 3932160 | bytes 7864320 | tf_op jit(solution)/shard_map/convert.1
  307.6 3.5 %all-to-all-start.5 = ((bf16[4,256,384]{2,1,0:T(8,128)(2,1)}), bf16[4,256,384]{2,1,0:T(8,128)(2,1)S(1)}, u32[]{:S(2)}, u32[]{:S(2)}) async-start(bf16[4,256,384]{2,1,0:T(8,128)(2,1)} %bitcast.53), calls=%async_computation.5 | async-start | bytes 1572864 | tf_op jit(solution)/shard_map/all_to_all | solution.py:147
  312.8 10.4 %all-to-all-done.5 = bf16[4,256,384]{2,1,0:T(8,128)(2,1)S(1)} async-done(((bf16[4,256,384]{2,1,0:T(8,128)(2,1)}), bf16[4,256,384]{2,1,0:T(8,128)(2,1)S(1)}, u32[]{:S(2)}, u32[]{:S(2)}) %all-to-all-start.5) | async-done | bytes 786464 | tf_op jit(solution)/shard_map/all_to_all | solution.py:147
  323.2 3.5 %all-to-all-start.6 = ((bf16[4,256,384]{2,1,0:T(8,128)(2,1)}), bf16[4,256,384]{2,1,0:T(8,128)(2,1)S(1)}, u32[]{:S(2)}, u32[]{:S(2)}) async-start(bf16[4,256,384]{2,1,0:T(8,128)(2,1)} %bitcast.56), calls=%async_computation.6 | async-start | bytes 1572864 | tf_op jit(solution)/shard_map/all_to_all | solution.py:150
  327.5 1.9 collective-permute-start.3
  329.4 13.2 %collective-permute-done.3 = bf16[1,256,384]{1,2,0:T(8,128)(2,1)} collective-permute-done((bf16[1,256,384]{1,2,0:T(8,128)(2,1)}, bf16[1,256,384]{1,2,0:T(8,128)(2,1)}, u32[]{:S(2)}, u32[]{:S(2)}) %collective-permute-start.3) | collective-permute-done | bytes 196640 | tf_op jit(solution)/shard_map/ppermute | solution.py:136
  (116 shorter events, 48.9 us)
Async XLA Ops:
  0.6 5.9 %copy-start.6 = (bf16[256,1536]{1,0:T(8,128)(2,1)S(1)}, bf16[256,1536]{1,0:T(8,128)(2,1)}, u32[]{:S(2)}) copy-start(bf16[256,1536]{1,0:T(8,128)(2,1)} %param.9) | copy-start | bytes 2359300
  3.0 15.1 %all-to-all-start.2 = ((bf16[256,4,384]{0,2,1:T(8,128)(2,1)}), bf16[256,4,384]{0,2,1:T(8,128)(2,1)S(1)}, u32[]{:S(2)}, u32[]{:S(2)}) async-start(bf16[256,4,384]{0,2,1:T(8,128)(2,1)} %bitcast.33), calls=%async_computation.2 | async-start | bytes 1572864 | tf_op jit(solution)/shard_map/all_to_all | solution.py:96
  18.1 15.1 %all-to-all-start.1 = ((bf16[256,4,384]{0,2,1:T(8,128)(2,1)}), bf16[256,4,384]{0,2,1:T(8,128)(2,1)S(1)}, u32[]{:S(2)}, u32[]{:S(2)}) async-start(bf16[256,4,384]{0,2,1:T(8,128)(2,1)} %bitcast.30), calls=%async_computation.1 | async-start | bytes 1572864 | tf_op jit(solution)/shard_map/all_to_all | solution.py:95
  22.0 17.8 %copy-start.7 = (bf16[256,1536]{1,0:T(8,128)(2,1)S(1)}, bf16[256,1536]{1,0:T(8,128)(2,1)}, u32[]{:S(2)}) copy-start(bf16[256,1536]{1,0:T(8,128)(2,1)} %param.8) | copy-start | bytes 2359300
  33.6 10.8 %copy-start.9 = (s32[16,3]{0,1:T(4,128)S(1)}, s32[16,3]{0,1:T(4,128)}, u32[]{:S(2)}) copy-start(s32[16,3]{0,1:T(4,128)} %param.12) | copy-start | bytes 580
  33.6 10.8 %copy-start.10 = (s32[16,3]{0,1:T(4,128)S(1)}, s32[16,3]{0,1:T(4,128)}, u32[]{:S(2)}) copy-start(s32[16,3]{0,1:T(4,128)} %param.13) | copy-start | bytes 580
  33.6 11.1 %copy-start.8 = (bf16[256,1536]{1,0:T(8,128)(2,1)S(1)}, bf16[256,1536]{1,0:T(8,128)(2,1)}, u32[]{:S(2)}) copy-start(bf16[256,1536]{1,0:T(8,128)(2,1)} %param.11) | copy-start | bytes 2359300
  35.0 36.1 %collective-permute-start.1 = (bf16[2,1024,384]{2,1,0:T(8,128)(2,1)}, bf16[2,1024,384]{2,1,0:T(8,128)(2,1)}, u32[]{:S(2)}, u32[]{:S(2)}) collective-permute-start(bf16[2,1024,384]{2,1,0:T(8,128)(2,1)} %pad_maximum_fusion.1), channel_id=1, source_target_pairs={{4,0},{8,4},{12,8},{5,1},{9,5},{13,9},{6,2},{10,6},{14,10},{7,3},{... | collective-permute-start | bytes 4718600 | tf_op jit(solution)/shard_map/ppermute | solution.py:33
  38.5 37.9 %collective-permute-start = (bf16[2,1024,384]{2,1,0:T(8,128)(2,1)}, bf16[2,1024,384]{2,1,0:T(8,128)(2,1)}, u32[]{:S(2)}, u32[]{:S(2)}) collective-permute-start(bf16[2,1024,384]{2,1,0:T(8,128)(2,1)} %pad_maximum_fusion.1), channel_id=1, source_target_pairs={{0,4},{4,8},{8,12},{1,5},{5,9},{9,13},{2,6},{6,10},{10,14},{3,7},{... | collective-permute-start | bytes 4718600 | tf_op jit(solution)/shard_map/ppermute | solution.py:31
  40.9 40.1 %all-to-all-start = ((bf16[256,4,384]{0,2,1:T(8,128)(2,1)}), bf16[256,4,384]{0,2,1:T(8,128)(2,1)S(1)}, u32[]{:S(2)}, u32[]{:S(2)}) async-start(bf16[256,4,384]{0,2,1:T(8,128)(2,1)} %bitcast.26), calls=%async_computation | async-start | bytes 1572864 | tf_op jit(solution)/shard_map/all_to_all | solution.py:94
  81.0 35.7 %all-to-all-start.3 = ((bf16[256,4,384]{0,2,1:T(8,128)(2,1)}), bf16[256,4,384]{0,2,1:T(8,128)(2,1)}, u32[]{:S(2)}, u32[]{:S(2)}) async-start(bf16[256,4,384]{0,2,1:T(8,128)(2,1)} %bitcast.38), calls=%async_computation.3 | async-start | bytes 1572864 | tf_op jit(solution)/shard_map/all_to_all | solution.py:97
  116.8 0.9 copy-start.3
  122.3 2.6 copy-start.2
  130.9 2.3 copy-start.1
  132.1 1.2 copy-start
  147.0 4.1 %copy-start.4 = (bf16[3,4,256,128]{2,3,0,1:T(8,128)(2,1)S(1)}, bf16[3,4,256,128]{2,3,0,1:T(8,128)(2,1)}, u32[]{:S(2)}) copy-start(bf16[3,4,256,128]{2,3,0,1:T(8,128)(2,1)} %copy-done.3) | copy-start | bytes 2359300 | tf_op jit(solution)/shard_map/while
  151.0 0.9 copy-start.3
  156.6 2.6 copy-start.2
  165.2 2.3 copy-start.1
  166.4 1.2 copy-start
  181.3 4.0 %copy-start.4 = (bf16[3,4,256,128]{2,3,0,1:T(8,128)(2,1)S(1)}, bf16[3,4,256,128]{2,3,0,1:T(8,128)(2,1)}, u32[]{:S(2)}) copy-start(bf16[3,4,256,128]{2,3,0,1:T(8,128)(2,1)} %copy-done.3) | copy-start | bytes 2359300 | tf_op jit(solution)/shard_map/while
  185.3 0.9 copy-start.3
  190.9 2.6 copy-start.2
  199.5 2.3 copy-start.1
  200.6 1.2 copy-start
  215.5 4.1 %copy-start.4 = (bf16[3,4,256,128]{2,3,0,1:T(8,128)(2,1)S(1)}, bf16[3,4,256,128]{2,3,0,1:T(8,128)(2,1)}, u32[]{:S(2)}) copy-start(bf16[3,4,256,128]{2,3,0,1:T(8,128)(2,1)} %copy-done.3) | copy-start | bytes 2359300 | tf_op jit(solution)/shard_map/while
  262.8 39.0 %collective-permute-start.6 = (bf16[2,1024,384]{1,2,0:T(8,128)(2,1)}, bf16[2,1024,384]{1,2,0:T(8,128)(2,1)}, u32[]{:S(2)}, u32[]{:S(2)}) collective-permute-start(bf16[2,1024,384]{1,2,0:T(8,128)(2,1)} %get-tuple-element.127), channel_id=1, source_target_pairs={{0,4},{4,8},{8,12},{1,5},{5,9},{9,13},{2,6},{6,10},{10,14},{3,7},{... | collective-permute-start | bytes 4718600 | tf_op jit(solution)/shard_map/ppermute | solution.py:43
  264.1 38.5 %collective-permute-start.5 = (bf16[2,1024,384]{1,2,0:T(8,128)(2,1)S(1)}, bf16[2,1024,384]{1,2,0:T(8,128)(2,1)}, u32[]{:S(2)}, u32[]{:S(2)}) collective-permute-start(bf16[2,1024,384]{1,2,0:T(8,128)(2,1)S(1)} %get-tuple-element.126), channel_id=1, source_target_pairs={{4,0},{8,4},{12,8},{5,1},{9,5},{13,9},{6,2},{10,6},{14,10},{7,3},{... | collective-permute-start | bytes 4718600 | tf_op jit(solution)/shard_map/ppermute | solution.py:43
  269.8 37.8 %all-to-all-start.4 = ((bf16[4,256,384]{1,2,0:T(8,128)(2,1)}), bf16[4,256,384]{1,2,0:T(8,128)(2,1)S(1)}, u32[]{:S(2)}, u32[]{:S(2)}) async-start(bf16[4,256,384]{1,2,0:T(8,128)(2,1)} %bitcast.48), calls=%async_computation.4 | async-start | bytes 1572864 | tf_op jit(solution)/shard_map/all_to_all | solution.py:146
  306.3 4.8 %copy-start.5 = (bf16[3,4,256,128]{2,3,0,1:T(8,128)(2,1)S(1)}, bf16[3,4,256,128]{2,3,0,1:T(8,128)(2,1)}, u32[]{:S(2)}) copy-start(bf16[3,4,256,128]{2,3,0,1:T(8,128)(2,1)} %get-tuple-element.64) | copy-start | bytes 2359300
  307.6 15.6 %all-to-all-start.5 = ((bf16[4,256,384]{2,1,0:T(8,128)(2,1)}), bf16[4,256,384]{2,1,0:T(8,128)(2,1)S(1)}, u32[]{:S(2)}, u32[]{:S(2)}) async-start(bf16[4,256,384]{2,1,0:T(8,128)(2,1)} %bitcast.53), calls=%async_computation.5 | async-start | bytes 1572864 | tf_op jit(solution)/shard_map/all_to_all | solution.py:147
  311.2 15.6 %collective-permute-start.2 = (bf16[1,256,384]{1,2,0:T(8,128)(2,1)S(1)}, bf16[1,256,384]{1,2,0:T(8,128)(2,1)S(1)}, u32[]{:S(2)}, u32[]{:S(2)}) collective-permute-start(bf16[1,256,384]{1,2,0:T(8,128)(2,1)S(1)} %constant_dynamic-slice_fusion.2), channel_id=1, source_target_pairs={{0,1},{1,2},{2,3},{3,0},{4,5},{5,6},{6,7},{7,4},{8,9},{9,10},{10,1... | collective-permute-start | bytes 589832 | tf_op jit(solution)/shard_map/ppermute | solution.py:136
  323.2 24.2 %all-to-all-start.6 = ((bf16[4,256,384]{2,1,0:T(8,128)(2,1)}), bf16[4,256,384]{2,1,0:T(8,128)(2,1)S(1)}, u32[]{:S(2)}, u32[]{:S(2)}) async-start(bf16[4,256,384]{2,1,0:T(8,128)(2,1)} %bitcast.56), calls=%async_computation.6 | async-start | bytes 1572864 | tf_op jit(solution)/shard_map/all_to_all | solution.py:150
  327.5 15.1 %collective-permute-start.3 = (bf16[1,256,384]{1,2,0:T(8,128)(2,1)}, bf16[1,256,384]{1,2,0:T(8,128)(2,1)}, u32[]{:S(2)}, u32[]{:S(2)}) collective-permute-start(bf16[1,256,384]{1,2,0:T(8,128)(2,1)} %get-tuple-element.133), channel_id=1, source_target_pairs={{0,2},{1,3},{2,0},{3,1},{4,6},{5,7},{6,4},{7,5},{8,10},{9,11},{10,... | collective-permute-start | bytes 589832 | tf_op jit(solution)/shard_map/ppermute | solution.py:136
  329.4 14.2 %collective-permute-start.4 = (bf16[1,256,384]{1,2,0:T(8,128)(2,1)S(1)}, bf16[1,256,384]{1,2,0:T(8,128)(2,1)S(1)}, u32[]{:S(2)}, u32[]{:S(2)}) collective-permute-start(bf16[1,256,384]{1,2,0:T(8,128)(2,1)S(1)} %get-tuple-element.132), channel_id=1, source_target_pairs={{0,3},{1,0},{2,1},{3,2},{4,7},{5,4},{6,5},{7,6},{8,11},{9,8},{10,9... | collective-permute-start | bytes 589832 | tf_op jit(solution)/shard_map/ppermute | solution.py:136
